TPU v7x, 128 devices: a whole 4x4x4 slice. The times are simulated.
128 devices in a mesh: pipe: 2 (over x_hi), tensor: 4 (over z), dp: 16 (over x_lo, y, core).
Axes of the slice: x: 4 (x_hi: 2, x_lo: 2; x = x_hi * 2 + x_lo), y: 4, z: 4, core: 2. Of those that a mesh axis runs over, the one named last changes fastest.
Arguments:
- tokens: bfloat16 [8192, 1024], P('dp', 'tensor'), may hold values from -6 to 6
- lengths: int32 [64, 4], P('dp'), may hold values from 1 to 85, 128 in all within a row
- ln_gain: bfloat16 [2, 2, 1024], P('pipe'), may hold values from 0.099609375 to 1.8984375
- ln_bias: bfloat16 [2, 2, 1024], P('pipe'), may hold values from -3 to 3
- joined_weight: bfloat16 [2, 1024, 3, 1024], P('pipe', None, None, 'tensor'), may hold values from -0.1875 to 0.1875
- joined_bias: bfloat16 [2, 3, 1024], P('pipe', None, 'tensor'), may hold values from -3 to 3
- dense_weight: bfloat16 [2, 1024, 1024], P('pipe', 'tensor'), may hold values from -0.5 to 0.5
- up_weight: bfloat16 [2, 1024, 4096], P('pipe', None, 'tensor'), may hold values from -0.1875 to 0.1875
- up_bias: bfloat16 [2, 4096], P('pipe', 'tensor'), may hold values from -3 to 3
- down_weight: bfloat16 [2, 4096, 1024], P('pipe', 'tensor'), may hold values from -0.09375 to 0.09375
- output_bias: bfloat16 [2, 2, 1024], P('pipe'), may hold values from -3 to 3
- cotangent: bfloat16 [8192, 1024], P('dp', 'tensor'), may hold values from -6 to 6
Outputs:
- section_out: bfloat16 [2, 8192, 1024], P('pipe', 'dp', 'tensor')
- input_grad: bfloat16 [2, 8192, 1024], P('pipe', 'dp', 'tensor')
- grad_ln_gain: float32 [2, 2, 1024], P('pipe')
- grad_ln_bias: float32 [2, 2, 1024], P('pipe')
- grad_joined: float32 [2, 1024, 3, 1024], P('pipe', None, None, 'tensor')
- grad_joined_bias: float32 [2, 3, 1024], P('pipe', None, 'tensor')
- grad_dense: float32 [2, 1024, 1024], P('pipe', 'tensor')
- grad_up: float32 [2, 1024, 4096], P('pipe', None, 'tensor')
- grad_up_bias: float32 [2, 4096], P('pipe', 'tensor')
- grad_down: float32 [2, 4096, 1024], P('pipe', 'tensor')
- grad_output_bias: float32 [2, 2, 1024], P('pipe')
Inputs may be any that keep to these rules, and one draw needn't show every extreme that they name: Row b gives, in order, the lengths of the 4 sequences that fill block b (tokens b * 128 to (b + 1) * 128 - 1); every row sums to 128.
All inputs are finite; a program needn't handle non-finite values.
Results may differ from a plain program's by a relative error of at most 0.035.
Values may be sent and summed in bfloat16 or wider, within the bound.
No kernel may reach another device: no remote copies, remote signals or barrier semaphores. Data moves between devices by JAX's collectives and lax.ppermute only.
A program may use at most 192 MiB of HBM per device.

v0:
```python
import jax
import jax.numpy as jnp
from jax import lax
from jax.sharding import PartitionSpec as P

HD = 64
ROT = 16
MB = 128
NMB = 4
EPSILON = 1e-05
MASKED = -1e30


def passed_along(x, axis, by):
    peers = lax.axis_size(axis)
    pairs = [(i, i + by) for i in range(peers) if 0 <= i + by < peers]
    return lax.ppermute(x, axis, pairs)


def as_sent(x):
    return jax.tree.map(lambda a: a.astype(jnp.bfloat16) if a.dtype == jnp.float32 else a, x)


def positions(lengths, block_rows):
    seq_count = lengths.shape[1]
    counter = jnp.arange(seq_count, dtype=jnp.int32)
    lower_tri = (counter[:, None] >= counter[None, :]).astype(jnp.int32)
    seg_ends = jnp.sum(lengths[:, None, :] * lower_tri[None, :, :], axis=2)
    starts = seg_ends - lengths
    row_index = jnp.arange(block_rows, dtype=jnp.int32)
    segment = jnp.sum((row_index[None, :, None] >= seg_ends[:, None, :]).astype(jnp.int32), axis=2)
    member = (segment[:, :, None] == counter[None, None, :]).astype(jnp.int32)
    place = row_index[None, :] - jnp.sum(member * starts[:, None, :], axis=2)
    return (segment, place)


def rotary(place):
    half_rot = ROT // 2
    inv_freq = jnp.power(10000.0, -2.0 * jnp.arange(half_rot, dtype=jnp.float32) / ROT)
    angles = place.astype(jnp.float32)[..., None] * inv_freq
    return (jnp.cos(angles), jnp.sin(angles))


def rotate(heads_in, cosv, sinv):
    half_rot = ROT // 2
    first_half = heads_in[..., :half_rot]
    second_half = heads_in[..., half_rot:ROT]
    cos_rows = cosv[:, None, :]
    sin_rows = sinv[:, None, :]
    return jnp.concatenate(
        [
            first_half * cos_rows - second_half * sin_rows,
            second_half * cos_rows + first_half * sin_rows,
            heads_in[..., ROT:],
        ],
        axis=-1,
    )


def rotate_back(heads_in, cosv, sinv):
    half_rot = ROT // 2
    first_half = heads_in[..., :half_rot]
    second_half = heads_in[..., half_rot:ROT]
    cos_rows = cosv[:, None, :]
    sin_rows = sinv[:, None, :]
    return jnp.concatenate(
        [
            first_half * cos_rows + second_half * sin_rows,
            second_half * cos_rows - first_half * sin_rows,
            heads_in[..., ROT:],
        ],
        axis=-1,
    )


def exact_gelu(values):
    return jax.nn.gelu(values, approximate=False)


def allowed_keys(segment):
    row_index = jnp.arange(segment.shape[0], dtype=jnp.int32)
    return (segment[:, None] == segment[None, :]) & (row_index[None, :] <= row_index[:, None])


def contract_rows(left, right):
    return lax.dot_general(
        left, right, (((0,), (0,)), ((), ())), preferred_element_type=jnp.float32
    )


def contract_cols(left, right):
    return lax.dot_general(
        left, right, (((1,), (1,)), ((), ())), preferred_element_type=jnp.float32
    )


def per_device(
    tokens,
    lengths,
    ln_gain,
    ln_bias,
    joined_weight,
    joined_bias,
    dense_weight,
    up_weight,
    up_bias,
    down_weight,
    output_bias,
    cotangent,
):
    leading = lax.axis_index("pipe") == 0
    model_width = joined_weight.shape[1]
    local_width = joined_weight.shape[3]
    local_heads = local_width // HD
    hidden_local = up_weight.shape[2]
    quarter = tokens.shape[1]
    score_scale = HD ** (-0.5)
    ln_gains = ln_gain[0].astype(jnp.float32)
    ln_shifts = ln_bias[0].astype(jnp.float32)
    joined_mat = joined_weight[0].reshape(model_width, 3 * local_width)
    joined_add = joined_bias[0].astype(jnp.float32).reshape(3 * local_width)
    dense_mat = dense_weight[0]
    up_mat = up_weight[0]
    up_add = up_bias[0].astype(jnp.float32)
    down_mat = down_weight[0]
    bias_sum = output_bias[0, 0].astype(jnp.float32) + output_bias[0, 1].astype(jnp.float32)
    gathered_rows = lax.all_gather(
        jnp.concatenate([tokens, cotangent], axis=0), "tensor", axis=1, tiled=True
    )
    input_rows = gathered_rows[: tokens.shape[0]]
    output_grads = gathered_rows[tokens.shape[0] :]
    segment_all, place_all = positions(lengths, MB)
    cos_all, sin_all = rotary(place_all)

    def pick(early_val, late_val):
        return jax.tree.map(
            lambda upper_val, lower_val: jnp.where(leading, upper_val, lower_val),
            early_val,
            late_val,
        )

    received = jnp.zeros((MB, model_width), jnp.bfloat16)
    tick_outputs = []
    tick_stored = []
    for section_tick in range(NMB + 1):
        early_block = min(section_tick, NMB - 1)
        late_block = max(section_tick - 1, 0)
        block_rows = jnp.where(
            leading, input_rows[early_block * MB : (early_block + 1) * MB], received
        )
        segment, cosv, sinv = pick(
            (segment_all[early_block], cos_all[early_block], sin_all[early_block]),
            (segment_all[late_block], cos_all[late_block], sin_all[late_block]),
        )
        inputs = block_rows.astype(jnp.float32)
        row_mean = jnp.mean(inputs, axis=1, keepdims=True)
        centred = inputs - row_mean
        forward_inv_scale = lax.rsqrt(jnp.mean(centred * centred, axis=1, keepdims=True) + EPSILON)
        forward_normed = centred * forward_inv_scale
        forward_h_attn = (forward_normed * ln_gains[0] + ln_shifts[0]).astype(jnp.bfloat16)
        forward_h_mlp = (forward_normed * ln_gains[1] + ln_shifts[1]).astype(jnp.bfloat16)
        joined_proj = (
            jnp.dot(forward_h_attn, joined_mat, preferred_element_type=jnp.float32) + joined_add
        )
        forward_block_len = block_rows.shape[0]
        forward_queries = rotate(
            joined_proj[:, :local_width].reshape(forward_block_len, local_heads, HD), cosv, sinv
        ).astype(jnp.bfloat16)
        forward_keys_rot = rotate(
            joined_proj[:, local_width : 2 * local_width].reshape(
                forward_block_len, local_heads, HD
            ),
            cosv,
            sinv,
        ).astype(jnp.bfloat16)
        forward_values = (
            joined_proj[:, 2 * local_width :]
            .reshape(forward_block_len, local_heads, HD)
            .astype(jnp.bfloat16)
        )
        forward_scores = (
            jnp.einsum(
                "qhd,khd->hqk",
                forward_queries,
                forward_keys_rot,
                preferred_element_type=jnp.float32,
            )
            * score_scale
        )
        forward_scores = jnp.where(allowed_keys(segment)[None], forward_scores, MASKED)
        row_top = jnp.max(forward_scores, axis=2, keepdims=True)
        exponent = jnp.exp(forward_scores - row_top)
        row_total = jnp.sum(exponent, axis=2, keepdims=True)
        forward_log_total = row_top + jnp.log(row_total)
        weights_low = (exponent / row_total).astype(jnp.bfloat16)
        forward_context = jnp.einsum(
            "hqk,khd->qhd", weights_low, forward_values, preferred_element_type=jnp.float32
        )
        forward_context = forward_context.reshape(forward_block_len, local_width).astype(
            jnp.bfloat16
        )
        forward_up_proj = (
            jnp.dot(forward_h_mlp, up_mat, preferred_element_type=jnp.float32) + up_add
        )
        forward_activated = exact_gelu(forward_up_proj).astype(jnp.bfloat16)
        partial_value = jnp.dot(forward_context, dense_mat, preferred_element_type=jnp.float32)
        partial_value = partial_value + jnp.dot(
            forward_activated, down_mat, preferred_element_type=jnp.float32
        )
        branches = lax.psum(partial_value.astype(jnp.bfloat16), "tensor").astype(jnp.float32)
        result = inputs + branches + bias_sum
        forward_stored = (
            forward_normed,
            forward_inv_scale,
            forward_h_attn,
            forward_h_mlp,
            forward_queries,
            forward_keys_rot,
            forward_values,
            forward_log_total,
            forward_context,
            forward_up_proj,
            forward_activated,
        )
        result, stored = (result, forward_stored)
        result_low = result.astype(jnp.bfloat16)
        tick_outputs.append(result_low)
        tick_stored.append((stored, segment, cosv, sinv))
        if section_tick < NMB:
            received = passed_along(result_low, "pipe", 1)
    column_start = lax.axis_index("tensor") * quarter
    section_rows = jnp.concatenate(
        [jnp.where(leading, tick_outputs[block], tick_outputs[block + 1]) for block in range(NMB)],
        axis=0,
    )
    section_out = lax.dynamic_slice_in_dim(section_rows, column_start, quarter, 1)[None]
    returned = jnp.zeros((MB, model_width), jnp.bfloat16)
    tick_grads = []
    totals = None
    for section_tick in range(NMB + 1):
        own_block = min(section_tick, NMB - 1)
        late_tick = max(section_tick - 1, 0)
        upper_tick = min(section_tick + 1, NMB)
        from_output = output_grads[own_block * MB : (own_block + 1) * MB]
        if section_tick == NMB:
            from_output = jnp.zeros_like(from_output)
        grad_rows = jnp.where(leading, returned, from_output)
        stored, segment, cosv, sinv = pick(tick_stored[late_tick], tick_stored[upper_tick])
        (
            normed,
            inv_scale,
            h_attn,
            h_mlp,
            queries,
            keys_rot,
            values,
            log_total,
            context,
            up_proj,
            activated,
        ) = stored
        block_len = grad_rows.shape[0]
        grad_wide = grad_rows.astype(jnp.float32)
        column_sum = jnp.sum(grad_wide, axis=0)
        backward_grad_dense = contract_rows(context, grad_rows)
        backward_grad_down = contract_rows(activated, grad_rows)
        d_context = contract_cols(grad_rows, dense_mat).astype(jnp.bfloat16)
        d_act = contract_cols(grad_rows, down_mat)
        unused, slope_back = jax.vjp(exact_gelu, up_proj)
        d_up = slope_back(d_act)[0].astype(jnp.bfloat16)
        grad_up_add = jnp.sum(d_up.astype(jnp.float32), axis=0)
        backward_grad_up = contract_rows(h_mlp, d_up)
        d_hmlp = contract_cols(d_up, up_mat)
        scores = (
            jnp.einsum("qhd,khd->hqk", queries, keys_rot, preferred_element_type=jnp.float32)
            * score_scale
        )
        scores = jnp.where(allowed_keys(segment)[None], scores, MASKED)
        weights_soft = jnp.exp(scores - log_total)
        d_context3 = d_context.reshape(block_len, local_heads, HD)
        d_values = jnp.einsum(
            "hqk,qhd->khd",
            weights_soft.astype(jnp.bfloat16),
            d_context3,
            preferred_element_type=jnp.float32,
        ).astype(jnp.bfloat16)
        d_weights = jnp.einsum(
            "qhd,khd->hqk", d_context3, values, preferred_element_type=jnp.float32
        )
        row_delta = jnp.sum(weights_soft * d_weights, axis=2, keepdims=True)
        d_scores = (weights_soft * (d_weights - row_delta)).astype(jnp.bfloat16)
        d_queries = (
            jnp.einsum("hqk,khd->qhd", d_scores, keys_rot, preferred_element_type=jnp.float32)
            * score_scale
        )
        d_keys = (
            jnp.einsum("hqk,qhd->khd", d_scores, queries, preferred_element_type=jnp.float32)
            * score_scale
        )
        d_queries = (
            rotate_back(d_queries, cosv, sinv).reshape(block_len, local_width).astype(jnp.bfloat16)
        )
        d_keys = (
            rotate_back(d_keys, cosv, sinv).reshape(block_len, local_width).astype(jnp.bfloat16)
        )
        d_joined = jnp.concatenate(
            [d_queries, d_keys, d_values.reshape(block_len, local_width)], axis=1
        )
        grad_joined_add = jnp.sum(d_joined.astype(jnp.float32), axis=0)
        backward_grad_joined = contract_rows(d_joined, h_attn)
        d_hattn = contract_cols(d_joined, joined_mat)
        d_hattn, d_hmlp = (
            lax.psum(d_hattn.astype(jnp.bfloat16), "tensor").astype(jnp.float32),
            lax.psum(d_hmlp.astype(jnp.bfloat16), "tensor").astype(jnp.float32),
        )
        grad_gains = jnp.concatenate(
            [jnp.sum(d_hattn * normed, axis=0), jnp.sum(d_hmlp * normed, axis=0)]
        )
        grad_shifts = jnp.concatenate([jnp.sum(d_hattn, axis=0), jnp.sum(d_hmlp, axis=0)])
        d_norm = d_hattn * ln_gains[0] + d_hmlp * ln_gains[1]
        grad_input = grad_wide + inv_scale * (
            d_norm
            - jnp.mean(d_norm, axis=1, keepdims=True)
            - normed * jnp.mean(d_norm * normed, axis=1, keepdims=True)
        )
        small_terms = jnp.concatenate(
            [grad_gains, grad_shifts, column_sum, column_sum, grad_joined_add, grad_up_add]
        )
        terms = (
            backward_grad_joined[None],
            backward_grad_dense[None],
            backward_grad_up[None],
            backward_grad_down[None],
            small_terms[None],
        )
        grad_input, terms = (grad_input, terms)
        grad_low = grad_input.astype(jnp.bfloat16)
        tick_grads.append(grad_low)
        if totals is None:
            totals = terms
        else:
            totals = jax.tree.map(lambda older, newer: older + newer, totals, terms)
        if section_tick < NMB:
            returned = passed_along(grad_low, "pipe", -1)
    small_rows = totals[4][0]
    small_pad = -small_rows.shape[0] % model_width
    small_rows = jnp.pad(small_rows, (0, small_pad)).reshape(-1, model_width)
    pieces = (totals[0][0], totals[1][0], totals[2][0], totals[3][0], small_rows)
    slab = jnp.concatenate([piece.astype(jnp.bfloat16) for piece in pieces], axis=0)
    slab = lax.psum(slab, "dp").astype(jnp.float32)
    summed = []
    offset = 0
    for piece in pieces:
        summed.append(slab[offset : offset + piece.shape[0]])
        offset = offset + piece.shape[0]
    grad_rows_all = jnp.concatenate(
        [jnp.where(leading, tick_grads[block + 1], tick_grads[block]) for block in range(NMB)],
        axis=0,
    )
    input_grad = lax.dynamic_slice_in_dim(grad_rows_all, column_start, quarter, 1)[None]
    grad_joined = summed[0].T.reshape(1, model_width, 3, local_width)
    grad_dense = summed[1][None]
    grad_up = summed[2][None]
    grad_down = summed[3][None]
    small_sum = summed[4].reshape(-1)
    offset = 0
    grad_ln_gain = small_sum[offset : offset + 2 * model_width].reshape(1, 2, model_width)
    offset = offset + 2 * model_width
    grad_ln_bias = small_sum[offset : offset + 2 * model_width].reshape(1, 2, model_width)
    offset = offset + 2 * model_width
    grad_output_bias = small_sum[offset : offset + 2 * model_width].reshape(1, 2, model_width)
    offset = offset + 2 * model_width
    grad_joined_bias = small_sum[offset : offset + 3 * local_width].reshape(1, 3, local_width)
    offset = offset + 3 * local_width
    grad_up_bias = small_sum[offset : offset + hidden_local].reshape(1, hidden_local)
    return (
        section_out,
        input_grad,
        grad_ln_gain,
        grad_ln_bias,
        grad_joined,
        grad_joined_bias,
        grad_dense,
        grad_up,
        grad_up_bias,
        grad_down,
        grad_output_bias,
    )


def solution(mesh):
    placed = (
        P("dp", "tensor"),
        P("dp", None),
        P("pipe", None, None),
        P("pipe", None, None),
        P("pipe", None, None, "tensor"),
        P("pipe", None, "tensor"),
        P("pipe", "tensor", None),
        P("pipe", None, "tensor"),
        P("pipe", "tensor"),
        P("pipe", "tensor", None),
        P("pipe", None, None),
        P("dp", "tensor"),
    )
    return jax.shard_map(
        per_device,
        mesh=mesh,
        in_specs=placed,
        out_specs=(
            P("pipe", "dp", "tensor"),
            P("pipe", "dp", "tensor"),
            P("pipe", None, None),
            P("pipe", None, None),
            P("pipe", None, None, "tensor"),
            P("pipe", None, "tensor"),
            P("pipe", "tensor", None),
            P("pipe", None, "tensor"),
            P("pipe", "tensor"),
            P("pipe", "tensor", None),
            P("pipe", None, None),
        ),
        check_vma=False,
    )
```

profile of v0, /device:TPU:25, one launch (start us, length us, event | category | flops | bytes accessed | tf_op | source)
XLA Modules:
  0.0 722.0 jit_solution(4068381418110488269)
XLA Ops:
  14.6 2.6 copy.141
  24.7 21.6 %all-gather.2.cloned.1.call-done = bf16[1024,1024]{1,0:T(8,128)(2,1)} async-done(((bf16[1024,256]{1,0:T(8,128)(2,1)}), bf16[1024,1024]{1,0:T(8,128)(2,1)}) %all-gather.2.cloned.1.call-update) | async-done | bytes 2097168 | tf_op jit(solution)/shard_map/all_gather | solution.py:127
  55.9 2.2 fusion.104
  58.8 41.0 %all-reduce.14.cloned.1.call-done = bf16[128,1024]{1,0:T(8,128)(2,1)} async-done(((bf16[128,1024]{1,0:T(8,128)(2,1)}), bf16[128,1024]{1,0:T(8,128)(2,1)}) %all-reduce.14.cloned.1.call-update) | async-done | bytes 262160 | tf_op jit(solution)/shard_map/psum | solution.py:210
  100.9 5.1 collective-permute-start
  117.9 2.9 fusion.50
  126.2 2.2 fusion.101
  128.4 3.6 convert_reduce_fusion.24
  134.9 3.9 fusion.386
  138.7 3.4 fusion.395
  142.9 5.4 fusion.377
  148.3 34.1 %all-reduce.26.cloned.1.call-done = (bf16[128,1024]{1,0:T(8,128)(2,1)}, bf16[128,1024]{1,0:T(8,128)(2,1)}, bf16[128,1024]{1,0:T(8,128)(2,1)}) async-done(((bf16[128,1024]{1,0:T(8,128)(2,1)}, bf16[128,1024]{1,0:T(8,128)(2,1)}, bf16[128,1024]{1,0:T(8,128)(2,1)}), (bf16[128,1024]{1,0:T(8,128)(2,1)}, bf16[128,1024]{1,0:T(8,128)(2,1)}, bf16[128,1024]{1,0:T(8,128)(2,1)})) %all-reduce.26.cloned.1.call-update) | async-done | bytes 786448 | tf_op jit(solution)/shard_map/psum | solution.py:210
  187.9 5.7 collective-permute-start.1
  194.3 2.4 collective-permute-done.1
  209.2 2.9 fusion.53
  223.4 2.5 convert_reduce_fusion.23
  231.0 4.0 fusion.384
  235.1 3.5 fusion.393
  239.3 4.5 fusion.375
  243.8 35.5 %all-reduce.24.cloned.1.call-done = (bf16[128,1024]{1,0:T(8,128)(2,1)}, bf16[128,1024]{1,0:T(8,128)(2,1)}, bf16[128,1024]{1,0:T(8,128)(2,1)}) async-done(((bf16[128,1024]{1,0:T(8,128)(2,1)}, bf16[128,1024]{1,0:T(8,128)(2,1)}, bf16[128,1024]{1,0:T(8,128)(2,1)}), (bf16[128,1024]{1,0:T(8,128)(2,1)}, bf16[128,1024]{1,0:T(8,128)(2,1)}, bf16[128,1024]{1,0:T(8,128)(2,1)})) %all-reduce.24.cloned.1.call-update) | async-done | bytes 786448 | tf_op jit(solution)/shard_map/psum | solution.py:210
  285.6 5.7 collective-permute-start.2
  294.4 2.5 convert_reduce_fusion.17
  306.5 2.9 fusion.56
  321.4 2.5 convert_reduce_fusion.22
  325.5 2.9 fusion.382
  328.7 2.2 fusion.95
  332.2 3.3 fusion.391
  336.3 4.4 fusion.373
  340.7 39.9 %all-reduce.22.cloned.1.call-done = (bf16[128,1024]{1,0:T(8,128)(2,1)}, bf16[128,1024]{1,0:T(8,128)(2,1)}, bf16[128,1024]{1,0:T(8,128)(2,1)}) async-done(((bf16[128,1024]{1,0:T(8,128)(2,1)}, bf16[128,1024]{1,0:T(8,128)(2,1)}, bf16[128,1024]{1,0:T(8,128)(2,1)}), (bf16[128,1024]{1,0:T(8,128)(2,1)}, bf16[128,1024]{1,0:T(8,128)(2,1)}, bf16[128,1024]{1,0:T(8,128)(2,1)})) %all-reduce.22.cloned.1.call-update) | async-done | bytes 786448 | tf_op jit(solution)/shard_map/psum | solution.py:210
  382.2 2.7 broadcast_select_fusion.2
  386.2 6.0 collective-permute-start.3
  417.7 2.4 fusion.389
  420.1 2.5 convert_reduce_fusion.21
  424.8 4.0 fusion.380
  428.9 4.4 fusion.371
  437.8 2.2 convolution_add_fusion.1
  442.2 40.8 %all-reduce.20.cloned.1.call-done = (bf16[128,1024]{1,0:T(8,128)(2,1)}, bf16[128,1024]{1,0:T(8,128)(2,1)}) async-done(((bf16[128,1024]{1,0:T(8,128)(2,1)}, bf16[128,1024]{1,0:T(8,128)(2,1)}), (bf16[128,1024]{1,0:T(8,128)(2,1)}, bf16[128,1024]{1,0:T(8,128)(2,1)})) %all-reduce.20.cloned.1.call-update) | async-done | bytes 524304 | tf_op jit(solution)/shard_map/psum | solution.py:314
  484.6 2.3 broadcast_select_fusion.1
  503.7 2.5 convert_reduce_fusion.20
  507.9 6.9 fusion.42
  519.2 2.7 fusion.41
  523.8 6.8 fusion
  530.6 23.6 %all-reduce.18.cloned.1.call-done = (bf16[128,1024]{1,0:T(8,128)(2,1)}, bf16[128,1024]{1,0:T(8,128)(2,1)}, bf16[128,1024]{1,0:T(8,128)(2,1)}) async-done(((bf16[128,1024]{1,0:T(8,128)(2,1)}, bf16[128,1024]{1,0:T(8,128)(2,1)}, bf16[128,1024]{1,0:T(8,128)(2,1)}), (bf16[128,1024]{1,0:T(8,128)(2,1)}, bf16[128,1024]{1,0:T(8,128)(2,1)}, bf16[128,1024]{1,0:T(8,128)(2,1)})) %all-reduce.18.cloned.1.call-update) | async-done | bytes 786448 | tf_op jit(solution)/shard_map/psum | solution.py:210
  560.9 135.7 %all-reduce.16.cloned.1.call-done = bf16[3080,1024]{1,0:T(8,128)(2,1)} async-done(((bf16[3080,1024]{1,0:T(8,128)(2,1)}), bf16[3080,1024]{1,0:T(8,128)(2,1)}) %all-reduce.16.cloned.1.call-update) | async-done | bytes 6307856 | tf_op jit(solution)/shard_map/psum | solution.py:350
  696.6 4.3 convert_element_type.684
  702.6 4.2 slice_bitcast_fusion
  707.4 3.4 slice.631
  710.9 3.5 copy.182
  (892 shorter events, 187.6 us)
Async XLA Ops:
  7.2 48.7 %copy-start = (bf16[1,1024,1024]{2,1,0:T(8,128)(2,1)S(1)}, bf16[1,1024,1024]{2,1,0:T(8,128)(2,1)}, u32[]{:S(2)}) copy-start(bf16[1,1024,1024]{2,1,0:T(8,128)(2,1)} %param.21) | copy-start | bytes 6291460
  7.2 39.1 %all-gather.2.cloned.1.call-start = ((), (), s32[]{:S(2)}) async-start(), calls=%async_computation | async-start | bytes 2621440 | tf_op jit(solution)/shard_map/all_gather | solution.py:127
  9.3 90.5 %all-reduce.14.cloned.1.call-start = ((), (), s32[]{:S(2)}) async-start(), calls=%async_computation.1 | async-start | bytes 524288 | tf_op jit(solution)/shard_map/psum | solution.py:210
  12.9 36.3 %copy-start.178 = (f32[128,8]{0,1:T(8,128)}, f32[128,8]{0,1:T(8,128)S(1)}, u32[]{:S(2)}) copy-start(f32[128,8]{0,1:T(8,128)S(1)} %get-tuple-element.105) | copy-start | bytes 12292
  14.1 35.1 %copy-start.179 = (f32[128,8]{0,1:T(8,128)}, f32[128,8]{0,1:T(8,128)S(1)}, u32[]{:S(2)}) copy-start(f32[128,8]{0,1:T(8,128)S(1)} %get-tuple-element.103) | copy-start | bytes 12292
  17.2 34.2 %copy-start.95 = (f32[768]{0:T(1024)}, f32[768]{0:T(1024)S(1)}, u32[]{:S(2)}) copy-start(f32[768]{0:T(1024)S(1)} %reshape.1267) | copy-start | bytes 9220
  17.3 35.7 %copy-start.99 = (f32[1,1024]{1,0:T(1,128)}, f32[1,1024]{1,0:T(1,128)S(1)}, u32[]{:S(2)}) copy-start(f32[1,1024]{1,0:T(1,128)S(1)} %add.657) | copy-start | bytes 12292
  24.7 33.4 %copy-start.182 = (f32[128,8]{0,1:T(8,128)}, f32[128,8]{0,1:T(8,128)S(1)}, u32[]{:S(2)}) copy-start(f32[128,8]{0,1:T(8,128)S(1)} %get-tuple-element.109) | copy-start | bytes 12292
  24.7 33.5 %copy-start.185 = (f32[128,8]{0,1:T(8,128)}, f32[128,8]{0,1:T(8,128)S(1)}, u32[]{:S(2)}) copy-start(f32[128,8]{0,1:T(8,128)S(1)} %get-tuple-element.215) | copy-start | bytes 12292
  55.9 50.2 %copy-start.281 = (s32[128]{0:T(128)S(1)}, s32[128]{0:T(128)}, u32[]{:S(2)}) copy-start(s32[128]{0:T(128)} %get-tuple-element.106) | copy-start | bytes 1540
  55.9 50.2 %copy-start.282 = (s32[128]{0:T(128)S(1)}, s32[128]{0:T(128)}, u32[]{:S(2)}) copy-start(s32[128]{0:T(128)} %get-tuple-element.246) | copy-start | bytes 1540
  58.1 124.3 %all-reduce.26.cloned.1.call-start = ((), (), s32[]{:S(2)}) async-start(), calls=%async_computation.7 | async-start | bytes 1572864 | tf_op jit(solution)/shard_map/psum | solution.py:210
  58.2 48.6 %copy-start.90 = (f32[1,1,1024]{2,1,0:T(1,128)}, f32[1,1,1024]{2,1,0:T(1,128)S(1)}, u32[]{:S(2)}) copy-start(f32[1,1,1024]{2,1,0:T(1,128)S(1)} %convert_add_fusion.10) | copy-start | bytes 12292
  100.9 7.9 %collective-permute-start = (bf16[128,1024]{1,0:T(8,128)(2,1)S(1)}, bf16[128,1024]{1,0:T(8,128)(2,1)S(1)}, u32[]{:S(2)}, u32[]{:S(2)}) collective-permute-start(bf16[128,1024]{1,0:T(8,128)(2,1)S(1)} %fusion.193), channel_id=1, source_target_pairs={{0,64},{1,65},{2,66},{3,67},{4,68},{5,69},{6,70},{7,71},{8,72},{9,... | collective-permute-start | bytes 786440 | tf_op jit(solution)/shard_map/ppermute | solution.py:17
  134.8 144.6 %all-reduce.24.cloned.1.call-start = ((), (), s32[]{:S(2)}) async-start(), calls=%async_computation.6 | async-start | bytes 1572864 | tf_op jit(solution)/shard_map/psum | solution.py:210
  142.8 39.6 %copy-start.132 = (f32[128]{0:T(128)S(1)}, f32[128]{0:T(128)}, u32[]{:S(2)}) copy-start(f32[128]{0:T(128)} %copy-done.130) | copy-start | bytes 1540
  142.8 39.6 %copy-start.137 = (f32[128]{0:T(128)S(1)}, f32[128]{0:T(128)}, u32[]{:S(2)}) copy-start(f32[128]{0:T(128)} %copy-done.135) | copy-start | bytes 1540
  142.8 39.6 %copy-start.188 = (f32[128]{0:T(128)S(1)}, f32[128]{0:T(128)}, u32[]{:S(2)}) copy-start(f32[128]{0:T(128)} %copy-done.186) | copy-start | bytes 1540
  142.9 39.6 %copy-start.203 = (f32[128]{0:T(128)S(1)}, f32[128]{0:T(128)}, u32[]{:S(2)}) copy-start(f32[128]{0:T(128)} %copy-done.201) | copy-start | bytes 1540
  142.9 41.3 %copy-start.279 = (f32[128]{0:T(128)S(1)}, f32[128]{0:T(128)}, u32[]{:S(2)}) copy-start(f32[128]{0:T(128)} %get-tuple-element.267) | copy-start | bytes 1540
  148.3 38.7 %copy-start.91 = (f32[1,1,1024]{2,1,0:T(1,128)S(1)}, f32[1,1,1024]{2,1,0:T(1,128)}, u32[]{:S(2)}) copy-start(f32[1,1,1024]{2,1,0:T(1,128)} %copy-done.90) | copy-start | bytes 12292
  185.7 8.6 %collective-permute-start.4 = (bf16[128,1024]{1,0:T(8,128)(2,1)S(1)}, bf16[128,1024]{1,0:T(8,128)(2,1)S(1)}, u32[]{:S(2)}, u32[]{:S(2)}) collective-permute-start(bf16[128,1024]{1,0:T(8,128)(2,1)S(1)} %fusion.187), channel_id=1, source_target_pairs={{64,0},{65,1},{66,2},{67,3},{68,4},{69,5},{70,6},{71,7},{72,8},{73... | collective-permute-start | bytes 786440 | tf_op jit(solution)/shard_map/ppermute | solution.py:17
  187.9 8.8 %collective-permute-start.1 = (bf16[128,1024]{1,0:T(8,128)(2,1)S(1)}, bf16[128,1024]{1,0:T(8,128)(2,1)S(1)}, u32[]{:S(2)}, u32[]{:S(2)}) collective-permute-start(bf16[128,1024]{1,0:T(8,128)(2,1)S(1)} %get-tuple-element.133), channel_id=1, source_target_pairs={{0,64},{1,65},{2,66},{3,67},{4,68},{5,69},{6,70},{7,71},{8,72},{9,... | collective-permute-start | bytes 786440 | tf_op jit(solution)/shard_map/ppermute | solution.py:17
  198.6 82.6 %copy-start.21 = (bf16[128,1024]{1,0:T(8,128)(2,1)}, bf16[128,1024]{1,0:T(8,128)(2,1)S(1)}, u32[]{:S(2)}) copy-start(bf16[128,1024]{1,0:T(8,128)(2,1)S(1)} %get-tuple-element.91) | copy-start | bytes 786436
  230.9 149.6 %all-reduce.22.cloned.1.call-start = ((), (), s32[]{:S(2)}) async-start(), calls=%async_computation.5 | async-start | bytes 1572864 | tf_op jit(solution)/shard_map/psum | solution.py:210
  239.3 40.1 %copy-start.142 = (f32[128]{0:T(128)S(1)}, f32[128]{0:T(128)}, u32[]{:S(2)}) copy-start(f32[128]{0:T(128)} %copy-done.140) | copy-start | bytes 1540
  239.3 40.1 %copy-start.146 = (f32[128]{0:T(128)S(1)}, f32[128]{0:T(128)}, u32[]{:S(2)}) copy-start(f32[128]{0:T(128)} %copy-done.144) | copy-start | bytes 1540
  239.3 40.1 %copy-start.190 = (f32[128]{0:T(128)S(1)}, f32[128]{0:T(128)}, u32[]{:S(2)}) copy-start(f32[128]{0:T(128)} %copy-done.186) | copy-start | bytes 1540
  239.3 40.1 %copy-start.205 = (f32[128]{0:T(128)S(1)}, f32[128]{0:T(128)}, u32[]{:S(2)}) copy-start(f32[128]{0:T(128)} %copy-done.201) | copy-start | bytes 1540
  239.3 41.8 %copy-start.278 = (f32[128]{0:T(128)S(1)}, f32[128]{0:T(128)}, u32[]{:S(2)}) copy-start(f32[128]{0:T(128)} %get-tuple-element.265) | copy-start | bytes 1540
  243.8 40.8 %copy-start.92 = (f32[1,1,1024]{2,1,0:T(1,128)S(1)}, f32[1,1,1024]{2,1,0:T(1,128)}, u32[]{:S(2)}) copy-start(f32[1,1,1024]{2,1,0:T(1,128)} %copy-done.90) | copy-start | bytes 12292
  283.2 9.5 %collective-permute-start.5 = (bf16[128,1024]{1,0:T(8,128)(2,1)S(1)}, bf16[128,1024]{1,0:T(8,128)(2,1)S(1)}, u32[]{:S(2)}, u32[]{:S(2)}) collective-permute-start(bf16[128,1024]{1,0:T(8,128)(2,1)S(1)} %get-tuple-element.101), channel_id=1, source_target_pairs={{64,0},{65,1},{66,2},{67,3},{68,4},{69,5},{70,6},{71,7},{72,8},{73... | collective-permute-start | bytes 786440 | tf_op jit(solution)/shard_map/ppermute | solution.py:17
  285.6 8.8 %collective-permute-start.2 = (bf16[128,1024]{1,0:T(8,128)(2,1)S(1)}, bf16[128,1024]{1,0:T(8,128)(2,1)S(1)}, u32[]{:S(2)}, u32[]{:S(2)}) collective-permute-start(bf16[128,1024]{1,0:T(8,128)(2,1)S(1)} %get-tuple-element.128), channel_id=1, source_target_pairs={{0,64},{1,65},{2,66},{3,67},{4,68},{5,69},{6,70},{7,71},{8,72},{9,... | collective-permute-start | bytes 786440 | tf_op jit(solution)/shard_map/ppermute | solution.py:17
  332.1 150.8 %all-reduce.20.cloned.1.call-start = ((), (), s32[]{:S(2)}) async-start(), calls=%async_computation.4 | async-start | bytes 1048576 | tf_op jit(solution)/shard_map/psum | solution.py:314
  336.3 44.3 %copy-start.118 = (f32[128]{0:T(128)S(1)}, f32[128]{0:T(128)}, u32[]{:S(2)}) copy-start(f32[128]{0:T(128)} %copy-done.116) | copy-start | bytes 1540
  336.3 44.3 %copy-start.122 = (f32[128]{0:T(128)S(1)}, f32[128]{0:T(128)}, u32[]{:S(2)}) copy-start(f32[128]{0:T(128)} %copy-done.120) | copy-start | bytes 1540
  336.3 44.3 %copy-start.134 = (f32[128]{0:T(128)S(1)}, f32[128]{0:T(128)}, u32[]{:S(2)}) copy-start(f32[128]{0:T(128)} %copy-done.130) | copy-start | bytes 1540
  336.3 44.3 %copy-start.139 = (f32[128]{0:T(128)S(1)}, f32[128]{0:T(128)}, u32[]{:S(2)}) copy-start(f32[128]{0:T(128)} %copy-done.135) | copy-start | bytes 1540
  336.3 45.9 %copy-start.93 = (f32[1,1,1024]{2,1,0:T(1,128)S(1)}, f32[1,1,1024]{2,1,0:T(1,128)}, u32[]{:S(2)}) copy-start(f32[1,1,1024]{2,1,0:T(1,128)} %copy-done.90) | copy-start | bytes 12292
  336.3 45.9 %copy-start.277 = (f32[128]{0:T(128)S(1)}, f32[128]{0:T(128)}, u32[]{:S(2)}) copy-start(f32[128]{0:T(128)} %get-tuple-element.263) | copy-start | bytes 1540
  384.9 8.6 %collective-permute-start.6 = (bf16[128,1024]{1,0:T(8,128)(2,1)S(1)}, bf16[128,1024]{1,0:T(8,128)(2,1)S(1)}, u32[]{:S(2)}, u32[]{:S(2)}) collective-permute-start(bf16[128,1024]{1,0:T(8,128)(2,1)S(1)} %get-tuple-element.99), channel_id=1, source_target_pairs={{64,0},{65,1},{66,2},{67,3},{68,4},{69,5},{70,6},{71,7},{72,8},{73... | collective-permute-start | bytes 786440 | tf_op jit(solution)/shard_map/ppermute | solution.py:17
  386.2 8.8 %collective-permute-start.3 = (bf16[128,1024]{1,0:T(8,128)(2,1)S(1)}, bf16[128,1024]{1,0:T(8,128)(2,1)S(1)}, u32[]{:S(2)}, u32[]{:S(2)}) collective-permute-start(bf16[128,1024]{1,0:T(8,128)(2,1)S(1)} %get-tuple-element.160), channel_id=1, source_target_pairs={{0,64},{1,65},{2,66},{3,67},{4,68},{5,69},{6,70},{7,71},{8,72},{9,... | collective-permute-start | bytes 786440 | tf_op jit(solution)/shard_map/ppermute | solution.py:17
  436.4 117.8 %all-reduce.18.cloned.1.call-start = ((), (), s32[]{:S(2)}) async-start(), calls=%async_computation.3 | async-start | bytes 1572864 | tf_op jit(solution)/shard_map/psum | solution.py:210
  486.9 8.8 %collective-permute-start.7 = (bf16[128,1024]{1,0:T(8,128)(2,1)S(1)}, bf16[128,1024]{1,0:T(8,128)(2,1)S(1)}, u32[]{:S(2)}, u32[]{:S(2)}) collective-permute-start(bf16[128,1024]{1,0:T(8,128)(2,1)S(1)} %get-tuple-element.97), channel_id=1, source_target_pairs={{64,0},{65,1},{66,2},{67,3},{68,4},{69,5},{70,6},{71,7},{72,8},{73... | collective-permute-start | bytes 786440 | tf_op jit(solution)/shard_map/ppermute | solution.py:17
  507.8 188.7 %all-reduce.16.cloned.1.call-start = ((), (), s32[]{:S(2)}) async-start(), calls=%async_computation.2 | async-start | bytes 12615680 | tf_op jit(solution)/shard_map/psum | solution.py:350
  523.7 32.1 %copy-start.169 = (f32[7936]{0:T(1024)S(1)}, f32[7936]{0:T(1024)}, u32[]{:S(2)}) copy-start(f32[7936]{0:T(1024)} %get-tuple-element.302) | copy-start | bytes 95236
  523.7 32.1 %copy-start.171 = (f32[7936]{0:T(1024)S(1)}, f32[7936]{0:T(1024)}, u32[]{:S(2)}) copy-start(f32[7936]{0:T(1024)} %copy-done.170) | copy-start | bytes 95236
  523.7 32.1 %copy-start.173 = (f32[7936]{0:T(1024)S(1)}, f32[7936]{0:T(1024)}, u32[]{:S(2)}) copy-start(f32[7936]{0:T(1024)} %get-tuple-element.304) | copy-start | bytes 95236
  (258 other events, 1405.2 us)
Sparse Core Ops, SparseCore 0:
  10.3 35.9 all-gather.1
  58.2 41.5 all-reduce.13
  134.9 47.4 all-reduce.25
  231.0 48.2 all-reduce.23
  332.3 48.2 all-reduce.21
  436.5 46.3 all-reduce.19
  507.9 46.2 all-reduce.17
  557.5 139.0 all-reduce.15
where the time goes:
time: 729 us; the launch traced here: 722 us
  waiting for transfers between devices  381 us (52%)
  matrix products  156 us (21%)
  other arithmetic  69 us (9%)
  local copies, waits for them, and re-layouts  68.4 us (9%)
  starting transfers between devices  28.3 us (4%)
  between operations  18.4 us (3%)
    psum x5, waiting for transfers between devices, per_device(): lax.psum(partial_value.astype(jnp.bfloat16), 'tensor').astype(jnp.float32)  174 us
    psum x1, waiting for transfers between devices, per_device(): slab = lax.psum(slab, 'dp').astype(jnp.float32)  136 us
    dot_general x20, matrix products, contract_rows(): lax.dot_general(left, right, (((0,), (0,)), ((), ())), preferred_element_...  68.6 us
    psum x1, waiting for transfers between devices, per_device(): lax.psum(d_hmlp.astype(jnp.bfloat16), 'tensor').astype(jnp.float32)  40.8 us
    dot_general x20, matrix products, contract_cols(): lax.dot_general(left, right, (((1,), (1,)), ((), ())), preferred_element_...  32.1 us
    ppermute x8, starting transfers between devices, passed_along(): return lax.ppermute(x, axis, pairs)  27.9 us
    all_gather x1, waiting for transfers between devices, per_device(): lax.all_gather(jnp.concatenate([tokens, cotangent], axis=0), 'tensor', ax...  21.6 us
    unnamed x619, local copies, waits for them, and re-layouts  20.5 us
  transfers between devices with their start and end apart: 16, of which 15 were waited for; matrix products, arithmetic and copies ran while one was open for 12% of the time, Pallas kernels for 0%

commit v1 on v0

--- a/solution.py
+++ b/solution.py
@@ -311,7 +311,9 @@
         d_hattn = contract_cols(d_joined, joined_mat)
         d_hattn, d_hmlp = (
             lax.psum(d_hattn.astype(jnp.bfloat16), "tensor").astype(jnp.float32),
-            lax.psum(d_hmlp.astype(jnp.bfloat16), "tensor").astype(jnp.float32),
+            jnp.sum(lax.all_gather(d_hmlp.astype(jnp.bfloat16), "tensor"), axis=0).astype(
+                jnp.float32
+            ),
         )
         grad_gains = jnp.concatenate(
             [jnp.sum(d_hattn * normed, axis=0), jnp.sum(d_hmlp * normed, axis=0)]

time: 729 us -> 813 us (1.12)
  waiting for transfers between devices: 381 us -> 443 us
  other arithmetic: 69 us -> 81 us
    all_gather x0 -> x5, waiting for transfers between devices: none -> 51.1 us  [per_device(): lax.all_gather(d_hmlp.astype(jnp.bfloat16), 'tensor')]
    ppermute x8, waiting for transfers between devices: 9.19 us -> 19.7 us  [passed_along(): return lax.ppermute(x, axis, pairs)]
    reduce_sum x0 -> x5, other arithmetic: none -> 9.43 us  [per_device(): jnp.sum(lax.all_gather(d_hmlp.astype(jnp.bfloat16), 'tensor'), axis=0)]
    unnamed x619 -> x631, local copies, waits for them, and re-layouts: 20.5 us -> 21.7 us
  transfers between devices with their start and end apart: 16 -> 21, of which waited for: 15 -> 18; matrix products, arithmetic and copies ran while one was open for 12% -> 19% of each run, Pallas kernels for 0% -> 0%
where the time goes in v1:
time: 813 us; the launch traced here: 803 us
  waiting for transfers between devices  443 us (54%)
  matrix products  159 us (20%)
  other arithmetic  81 us (10%)
  local copies, waits for them, and re-layouts  72.1 us (9%)
  starting transfers between devices  28.7 us (4%)
  between operations  18.1 us (2%)
    psum x5, waiting for transfers between devices, per_device(): lax.psum(partial_value.astype(jnp.bfloat16), 'tensor').astype(jnp.float32)  174 us
    psum x1, waiting for transfers between devices, per_device(): slab = lax.psum(slab, 'dp').astype(jnp.float32)  136 us
    dot_general x20, matrix products, contract_rows(): lax.dot_general(left, right, (((0,), (0,)), ((), ())), preferred_element_...  71.4 us
    all_gather x5, waiting for transfers between devices, per_device(): lax.all_gather(d_hmlp.astype(jnp.bfloat16), 'tensor')  51.1 us
    psum x1, waiting for transfers between devices, per_device(): lax.psum(d_hattn.astype(jnp.bfloat16), 'tensor').astype(jnp.float32)  41.2 us
    dot_general x20, matrix products, contract_cols(): lax.dot_general(left, right, (((1,), (1,)), ((), ())), preferred_element_...  34.4 us
    ppermute x8, starting transfers between devices, passed_along(): return lax.ppermute(x, axis, pairs)  26.7 us
    unnamed x631, local copies, waits for them, and re-layouts  21.7 us
  transfers between devices with their start and end apart: 21, of which 18 were waited for; matrix products, arithmetic and copies ran while one was open for 19% of the time, Pallas kernels for 0%

profile of v1, /device:TPU:25, one launch (start us, length us, event | category | flops | bytes accessed | tf_op | source)
XLA Modules:
  0.0 802.5 jit_solution(4029072418604809444)
XLA Ops:
  15.3 2.6 copy.141
  25.4 21.1 %all-gather.12.cloned.1.call-done = bf16[1024,1024]{1,0:T(8,128)(2,1)} async-done(((bf16[1024,256]{1,0:T(8,128)(2,1)}), bf16[1024,1024]{1,0:T(8,128)(2,1)}) %all-gather.12.cloned.1.call-update) | async-done | bytes 2097168 | tf_op jit(solution)/shard_map/all_gather | solution.py:127
  59.0 40.7 %all-reduce.13.cloned.1.call-done = bf16[128,1024]{1,0:T(8,128)(2,1)} async-done(((bf16[128,1024]{1,0:T(8,128)(2,1)}), bf16[128,1024]{1,0:T(8,128)(2,1)}) %all-reduce.13.cloned.1.call-update) | async-done | bytes 262160 | tf_op jit(solution)/shard_map/psum | solution.py:210
  100.9 5.3 collective-permute-start
  110.8 2.9 fusion.50
  124.1 3.7 convert_reduce_fusion.24
  129.7 3.3 fusion.395
  133.0 3.9 fusion.386
  136.9 5.5 fusion.377
  142.4 27.2 %all-reduce.25.cloned.1.call-done = (bf16[128,1024]{1,0:T(8,128)(2,1)}, bf16[128,1024]{1,0:T(8,128)(2,1)}) async-done(((bf16[128,1024]{1,0:T(8,128)(2,1)}, bf16[128,1024]{1,0:T(8,128)(2,1)}), (bf16[128,1024]{1,0:T(8,128)(2,1)}, bf16[128,1024]{1,0:T(8,128)(2,1)})) %all-reduce.25.cloned.1.call-update) | async-done | bytes 524304 | tf_op jit(solution)/shard_map/psum | solution.py:210
  171.4 5.3 collective-permute-start.1
  176.7 20.8 %all-gather.14.cloned.1.call-done = bf16[512,1024]{1,0:T(8,128)(2,1)} async-done(((bf16[128,1024]{1,0:T(8,128)(2,1)}), bf16[512,1024]{1,0:T(8,128)(2,1)}) %all-gather.14.cloned.1.call-update) | async-done | bytes 1048592 | tf_op jit(solution)/shard_map/all_gather | solution.py:314
  203.4 8.2 %collective-permute-done.4 = bf16[128,1024]{1,0:T(8,128)(2,1)S(1)} collective-permute-done((bf16[128,1024]{1,0:T(8,128)(2,1)S(1)}, bf16[128,1024]{1,0:T(8,128)(2,1)S(1)}, u32[]{:S(2)}, u32[]{:S(2)}) %collective-permute-start.4) | collective-permute-done | bytes 262176 | tf_op jit(solution)/shard_map/ppermute | solution.py:17
  240.4 3.7 convert_reduce_fusion.23
  246.5 3.5 fusion.393
  250.0 4.0 fusion.384
  254.0 4.5 fusion.375
  258.5 23.7 %all-reduce.23.cloned.1.call-done = (bf16[128,1024]{1,0:T(8,128)(2,1)}, bf16[128,1024]{1,0:T(8,128)(2,1)}) async-done(((bf16[128,1024]{1,0:T(8,128)(2,1)}, bf16[128,1024]{1,0:T(8,128)(2,1)}), (bf16[128,1024]{1,0:T(8,128)(2,1)}, bf16[128,1024]{1,0:T(8,128)(2,1)})) %all-reduce.23.cloned.1.call-update) | async-done | bytes 524304 | tf_op jit(solution)/shard_map/psum | solution.py:210
  284.2 5.2 collective-permute-start.2
  289.4 20.7 %all-gather.16.cloned.1.call-done = bf16[512,1024]{1,0:T(8,128)(2,1)} async-done(((bf16[128,1024]{1,0:T(8,128)(2,1)}), bf16[512,1024]{1,0:T(8,128)(2,1)}) %all-gather.16.cloned.1.call-update) | async-done | bytes 1048592 | tf_op jit(solution)/shard_map/all_gather | solution.py:314
  325.9 2.5 convert_reduce_fusion.17
  354.2 2.5 convert_reduce_fusion.22
  367.8 6.2 fusion.373
  374.5 3.2 fusion.391
  377.8 2.9 fusion.382
  380.7 3.0 all-gather.18.cloned.1.call-done
  385.9 43.0 %all-reduce.21.cloned.1.call-done = (bf16[128,1024]{1,0:T(8,128)(2,1)}, bf16[128,1024]{1,0:T(8,128)(2,1)}) async-done(((bf16[128,1024]{1,0:T(8,128)(2,1)}, bf16[128,1024]{1,0:T(8,128)(2,1)}), (bf16[128,1024]{1,0:T(8,128)(2,1)}, bf16[128,1024]{1,0:T(8,128)(2,1)})) %all-reduce.21.cloned.1.call-update) | async-done | bytes 524304 | tf_op jit(solution)/shard_map/psum | solution.py:210
  430.6 2.7 broadcast_select_fusion.2
  434.6 5.5 collective-permute-start.3
  466.8 2.5 convert_reduce_fusion.21
  471.5 3.9 fusion.380
  478.3 3.4 fusion.389
  483.9 3.5 fusion.92
  487.4 4.4 fusion.371
  497.5 6.5 all-gather.20.cloned.1.call-done
  506.2 41.2 %all-reduce.15.cloned.1.call-done = bf16[128,1024]{1,0:T(8,128)(2,1)} async-done(((bf16[128,1024]{1,0:T(8,128)(2,1)}), bf16[128,1024]{1,0:T(8,128)(2,1)}) %all-reduce.15.cloned.1.call-update) | async-done | bytes 262160 | tf_op jit(solution)/shard_map/psum | solution.py:313
  549.2 2.3 broadcast_select_fusion.1
  554.1 5.9 collective-permute-done.7
  560.1 2.5 convert_reduce_fusion.20
  571.0 6.9 fusion.42
  582.3 2.7 fusion.41
  586.9 6.9 fusion
  595.5 39.7 %all-reduce.19.cloned.1.call-done = (bf16[128,1024]{1,0:T(8,128)(2,1)}, bf16[128,1024]{1,0:T(8,128)(2,1)}) async-done(((bf16[128,1024]{1,0:T(8,128)(2,1)}, bf16[128,1024]{1,0:T(8,128)(2,1)}), (bf16[128,1024]{1,0:T(8,128)(2,1)}, bf16[128,1024]{1,0:T(8,128)(2,1)})) %all-reduce.19.cloned.1.call-update) | async-done | bytes 524304 | tf_op jit(solution)/shard_map/psum | solution.py:210
  641.8 135.6 %all-reduce.17.cloned.1.call-done = bf16[3080,1024]{1,0:T(8,128)(2,1)} async-done(((bf16[3080,1024]{1,0:T(8,128)(2,1)}), bf16[3080,1024]{1,0:T(8,128)(2,1)}) %all-reduce.17.cloned.1.call-update) | async-done | bytes 6307856 | tf_op jit(solution)/shard_map/psum | solution.py:352
  777.4 4.3 convert_element_type.694
  783.4 4.2 slice_bitcast_fusion
  788.2 3.4 slice.631
  791.7 3.5 copy.182
  (924 shorter events, 213.6 us)
Async XLA Ops:
  7.2 48.9 %copy-start = (bf16[1,1024,1024]{2,1,0:T(8,128)(2,1)S(1)}, bf16[1,1024,1024]{2,1,0:T(8,128)(2,1)}, u32[]{:S(2)}) copy-start(bf16[1,1024,1024]{2,1,0:T(8,128)(2,1)} %param.21) | copy-start | bytes 6291460
  7.2 39.3 %all-gather.12.cloned.1.call-start = ((), (), s32[]{:S(2)}) async-start(), calls=%async_computation | async-start | bytes 2621440 | tf_op jit(solution)/shard_map/all_gather | solution.py:127
  9.3 90.5 %all-reduce.13.cloned.1.call-start = ((), (), s32[]{:S(2)}) async-start(), calls=%async_computation.1 | async-start | bytes 524288 | tf_op jit(solution)/shard_map/psum | solution.py:210
  56.1 50.1 %copy-start.288 = (s32[128]{0:T(128)S(1)}, s32[128]{0:T(128)}, u32[]{:S(2)}) copy-start(s32[128]{0:T(128)} %get-tuple-element.100) | copy-start | bytes 1540
  56.1 50.1 %copy-start.289 = (s32[128]{0:T(128)S(1)}, s32[128]{0:T(128)}, u32[]{:S(2)}) copy-start(s32[128]{0:T(128)} %get-tuple-element.240) | copy-start | bytes 1540
  58.3 51.9 %copy-start.274 = (f32[128]{0:T(128)S(1)}, f32[128]{0:T(128)}, u32[]{:S(2)}) copy-start(f32[128]{0:T(128)} %copy-done.273) | copy-start | bytes 1540
  58.3 52.5 %copy-start.92 = (f32[1,1024]{1,0:T(1,128)S(1)}, f32[1,1024]{1,0:T(1,128)}, u32[]{:S(2)}) copy-start(f32[1,1024]{1,0:T(1,128)} %copy-done.91) | copy-start | bytes 12292
  58.3 111.2 %all-reduce.25.cloned.1.call-start = ((), (), s32[]{:S(2)}) async-start(), calls=%async_computation.12 | async-start | bytes 1048576 | tf_op jit(solution)/shard_map/psum | solution.py:210
  58.4 111.2 %copy-start.87 = (f32[1,1,1024]{2,1,0:T(1,128)}, f32[1,1,1024]{2,1,0:T(1,128)S(1)}, u32[]{:S(2)}) copy-start(f32[1,1,1024]{2,1,0:T(1,128)S(1)} %convert_add_fusion.10) | copy-start | bytes 12292
  100.9 7.9 collective-permute-start
  109.9 89.0 %copy-start.132 = (f32[128]{0:T(128)}, f32[128]{0:T(128)S(1)}, u32[]{:S(2)}) copy-start(f32[128]{0:T(128)S(1)} %broadcast_multiply_fusion.13) | copy-start | bytes 1540
  110.8 88.2 %copy-start.135 = (f32[128]{0:T(128)}, f32[128]{0:T(128)S(1)}, u32[]{:S(2)}) copy-start(f32[128]{0:T(128)S(1)} %get-tuple-element.262) | copy-start | bytes 1540
  123.6 73.9 %all-gather.14.cloned.1.call-start = ((), (), s32[]{:S(2)}) async-start(), calls=%async_computation.4 | async-start | bytes 1310720 | tf_op jit(solution)/shard_map/all_gather | solution.py:314
  129.6 152.6 %all-reduce.23.cloned.1.call-start = ((), (), s32[]{:S(2)}) async-start(), calls=%async_computation.11 | async-start | bytes 1048576 | tf_op jit(solution)/shard_map/psum | solution.py:210
  171.4 32.0 %collective-permute-start.1 = (bf16[128,1024]{1,0:T(8,128)(2,1)S(1)}, bf16[128,1024]{1,0:T(8,128)(2,1)}, u32[]{:S(2)}, u32[]{:S(2)}) collective-permute-start(bf16[128,1024]{1,0:T(8,128)(2,1)S(1)} %get-tuple-element.127), channel_id=1, source_target_pairs={{0,64},{1,65},{2,66},{3,67},{4,68},{5,69},{6,70},{7,71},{8,72},{9,... | collective-permute-start | bytes 786440 | tf_op jit(solution)/shard_map/ppermute | solution.py:17
  202.0 9.6 %collective-permute-start.4 = (bf16[128,1024]{1,0:T(8,128)(2,1)S(1)}, bf16[128,1024]{1,0:T(8,128)(2,1)S(1)}, u32[]{:S(2)}, u32[]{:S(2)}) collective-permute-start(bf16[128,1024]{1,0:T(8,128)(2,1)S(1)} %fusion.187), channel_id=1, source_target_pairs={{64,0},{65,1},{66,2},{67,3},{68,4},{69,5},{70,6},{71,7},{72,8},{73... | collective-permute-start | bytes 786440 | tf_op jit(solution)/shard_map/ppermute | solution.py:17
  213.5 100.6 %copy-start.24 = (bf16[128,1024]{1,0:T(8,128)(2,1)}, bf16[128,1024]{1,0:T(8,128)(2,1)S(1)}, u32[]{:S(2)}) copy-start(bf16[128,1024]{1,0:T(8,128)(2,1)S(1)} %get-tuple-element.85) | copy-start | bytes 786436
  240.2 70.0 %all-gather.16.cloned.1.call-start = ((), (), s32[]{:S(2)}) async-start(), calls=%async_computation.5 | async-start | bytes 1310720 | tf_op jit(solution)/shard_map/all_gather | solution.py:314
  246.4 137.4 %all-gather.18.cloned.1.call-start = ((), (), s32[]{:S(2)}) async-start(), calls=%async_computation.6 | async-start | bytes 1310720 | tf_op jit(solution)/shard_map/all_gather | solution.py:314
  258.5 53.8 %copy-start.140 = (f32[128]{0:T(128)S(1)}, f32[128]{0:T(128)}, u32[]{:S(2)}) copy-start(f32[128]{0:T(128)} %copy-done.138) | copy-start | bytes 1540
  258.5 53.8 %copy-start.145 = (f32[128]{0:T(128)S(1)}, f32[128]{0:T(128)}, u32[]{:S(2)}) copy-start(f32[128]{0:T(128)} %copy-done.143) | copy-start | bytes 1540
  258.5 53.9 %copy-start.196 = (f32[128]{0:T(128)S(1)}, f32[128]{0:T(128)}, u32[]{:S(2)}) copy-start(f32[128]{0:T(128)} %copy-done.193) | copy-start | bytes 1540
  258.5 53.9 %copy-start.210 = (f32[128]{0:T(128)S(1)}, f32[128]{0:T(128)}, u32[]{:S(2)}) copy-start(f32[128]{0:T(128)} %copy-done.207) | copy-start | bytes 1540
  284.2 39.8 %collective-permute-start.2 = (bf16[128,1024]{1,0:T(8,128)(2,1)}, bf16[128,1024]{1,0:T(8,128)(2,1)}, u32[]{:S(2)}, u32[]{:S(2)}) collective-permute-start(bf16[128,1024]{1,0:T(8,128)(2,1)} %get-tuple-element.122), channel_id=1, source_target_pairs={{0,64},{1,65},{2,66},{3,67},{4,68},{5,69},{6,70},{7,71},{8,72},{9,... | collective-permute-start | bytes 786440 | tf_op jit(solution)/shard_map/ppermute | solution.py:17
  316.3 9.6 %collective-permute-start.5 = (bf16[128,1024]{1,0:T(8,128)(2,1)S(1)}, bf16[128,1024]{1,0:T(8,128)(2,1)S(1)}, u32[]{:S(2)}, u32[]{:S(2)}) collective-permute-start(bf16[128,1024]{1,0:T(8,128)(2,1)S(1)} %get-tuple-element.95), channel_id=1, source_target_pairs={{64,0},{65,1},{66,2},{67,3},{68,4},{69,5},{70,6},{71,7},{72,8},{73... | collective-permute-start | bytes 786440 | tf_op jit(solution)/shard_map/ppermute | solution.py:17
  358.9 70.0 %all-reduce.21.cloned.1.call-start = ((), (), s32[]{:S(2)}) async-start(), calls=%async_computation.10 | async-start | bytes 1048576 | tf_op jit(solution)/shard_map/psum | solution.py:210
  374.0 130.0 %all-gather.20.cloned.1.call-start = ((), (), s32[]{:S(2)}) async-start(), calls=%async_computation.7 | async-start | bytes 1310720 | tf_op jit(solution)/shard_map/all_gather | solution.py:314
  377.7 51.2 %copy-start.113 = (f32[128]{0:T(128)S(1)}, f32[128]{0:T(128)}, u32[]{:S(2)}) copy-start(f32[128]{0:T(128)} %copy-done.111) | copy-start | bytes 1540
  377.8 51.2 %copy-start.117 = (f32[128]{0:T(128)S(1)}, f32[128]{0:T(128)}, u32[]{:S(2)}) copy-start(f32[128]{0:T(128)} %copy-done.115) | copy-start | bytes 1540
  377.8 51.2 %copy-start.134 = (f32[128]{0:T(128)S(1)}, f32[128]{0:T(128)}, u32[]{:S(2)}) copy-start(f32[128]{0:T(128)} %copy-done.132) | copy-start | bytes 1540
  377.8 51.2 %copy-start.137 = (f32[128]{0:T(128)S(1)}, f32[128]{0:T(128)}, u32[]{:S(2)}) copy-start(f32[128]{0:T(128)} %copy-done.135) | copy-start | bytes 1540
  380.7 49.9 %copy-start.89 = (f32[1,1,1024]{2,1,0:T(1,128)S(1)}, f32[1,1,1024]{2,1,0:T(1,128)}, u32[]{:S(2)}) copy-start(f32[1,1,1024]{2,1,0:T(1,128)} %copy-done.87) | copy-start | bytes 12292
  380.7 49.9 %copy-start.285 = (f32[128]{0:T(128)S(1)}, f32[128]{0:T(128)}, u32[]{:S(2)}) copy-start(f32[128]{0:T(128)} %get-tuple-element.257) | copy-start | bytes 1540
  433.4 8.6 %collective-permute-start.6 = (bf16[128,1024]{1,0:T(8,128)(2,1)S(1)}, bf16[128,1024]{1,0:T(8,128)(2,1)S(1)}, u32[]{:S(2)}, u32[]{:S(2)}) collective-permute-start(bf16[128,1024]{1,0:T(8,128)(2,1)S(1)} %get-tuple-element.93), channel_id=1, source_target_pairs={{64,0},{65,1},{66,2},{67,3},{68,4},{69,5},{70,6},{71,7},{72,8},{73... | collective-permute-start | bytes 786440 | tf_op jit(solution)/shard_map/ppermute | solution.py:17
  434.6 8.8 %collective-permute-start.3 = (bf16[128,1024]{1,0:T(8,128)(2,1)S(1)}, bf16[128,1024]{1,0:T(8,128)(2,1)S(1)}, u32[]{:S(2)}, u32[]{:S(2)}) collective-permute-start(bf16[128,1024]{1,0:T(8,128)(2,1)S(1)} %get-tuple-element.154), channel_id=1, source_target_pairs={{0,64},{1,65},{2,66},{3,67},{4,68},{5,69},{6,70},{7,71},{8,72},{9,... | collective-permute-start | bytes 786440 | tf_op jit(solution)/shard_map/ppermute | solution.py:17
  475.4 72.0 %all-reduce.15.cloned.1.call-start = ((), (), s32[]{:S(2)}) async-start(), calls=%async_computation.2 | async-start | bytes 524288 | tf_op jit(solution)/shard_map/psum | solution.py:313
  491.8 102.3 %all-gather.22.cloned.1.call-start = ((), (), s32[]{:S(2)}) async-start(), calls=%async_computation.8 | async-start | bytes 1310720 | tf_op jit(solution)/shard_map/all_gather | solution.py:314
  496.2 52.9 %copy-start.122 = (f32[128]{0:T(128)S(1)}, f32[128]{0:T(128)}, u32[]{:S(2)}) copy-start(f32[128]{0:T(128)} %copy-done.120) | copy-start | bytes 1540
  496.2 52.9 %copy-start.128 = (f32[128]{0:T(128)S(1)}, f32[128]{0:T(128)}, u32[]{:S(2)}) copy-start(f32[128]{0:T(128)} %copy-done.126) | copy-start | bytes 1540
  496.2 52.9 %copy-start.142 = (f32[128]{0:T(128)S(1)}, f32[128]{0:T(128)}, u32[]{:S(2)}) copy-start(f32[128]{0:T(128)} %copy-done.138) | copy-start | bytes 1540
  496.2 52.9 %copy-start.147 = (f32[128]{0:T(128)S(1)}, f32[128]{0:T(128)}, u32[]{:S(2)}) copy-start(f32[128]{0:T(128)} %copy-done.143) | copy-start | bytes 1540
  496.2 53.0 %copy-start.290 = (f32[128]{0:T(128)S(1)}, f32[128]{0:T(128)}, u32[]{:S(2)}) copy-start(f32[128]{0:T(128)} %get-tuple-element.256) | copy-start | bytes 1540
  504.0 48.8 %copy-start.213 = (f32[768]{0:T(1024)S(1)}, f32[768]{0:T(1024)}, u32[]{:S(2)}) copy-start(f32[768]{0:T(1024)} %convert_reduce_fusion.26) | copy-start | bytes 9220
  504.0 48.8 %copy-start.279 = (f32[1024]{0:T(1024)S(1)}, f32[1024]{0:T(1024)}, u32[]{:S(2)}) copy-start(f32[1024]{0:T(1024)} %get-tuple-element.288) | copy-start | bytes 12292
  504.0 48.8 %copy-start.281 = (f32[1024]{0:T(1024)S(1)}, f32[1024]{0:T(1024)}, u32[]{:S(2)}) copy-start(f32[1024]{0:T(1024)} %get-tuple-element.286) | copy-start | bytes 12292
  551.4 8.6 %collective-permute-start.7 = (bf16[128,1024]{1,0:T(8,128)(2,1)S(1)}, bf16[128,1024]{1,0:T(8,128)(2,1)S(1)}, u32[]{:S(2)}, u32[]{:S(2)}) collective-permute-start(bf16[128,1024]{1,0:T(8,128)(2,1)S(1)} %get-tuple-element.91), channel_id=1, source_target_pairs={{64,0},{65,1},{66,2},{67,3},{68,4},{69,5},{70,6},{71,7},{72,8},{73... | collective-permute-start | bytes 786440 | tf_op jit(solution)/shard_map/ppermute | solution.py:17
  564.8 70.4 %all-reduce.19.cloned.1.call-start = ((), (), s32[]{:S(2)}) async-start(), calls=%async_computation.9 | async-start | bytes 1048576 | tf_op jit(solution)/shard_map/psum | solution.py:210
  570.6 206.8 %all-reduce.17.cloned.1.call-start = ((), (), s32[]{:S(2)}) async-start(), calls=%async_computation.3 | async-start | bytes 12615680 | tf_op jit(solution)/shard_map/psum | solution.py:352
  (269 other events, 2000.4 us)
Sparse Core Ops, SparseCore 0:
  10.3 36.2 all-gather.11
  58.4 41.2 all-reduce.12
  123.7 45.7 all-reduce.24
  171.8 25.6 all-gather.13
  240.3 41.8 all-reduce.22
  284.4 25.6 all-gather.15
  359.0 24.6 all-gather.17
  386.3 42.6 all-reduce.20
  475.5 28.4 all-gather.19
  506.3 41.0 all-reduce.14
  564.9 25.3 all-gather.21
  592.6 42.6 all-reduce.18
  638.4 138.8 all-reduce.16
